TPU v7x, 128 devices: a whole 4x4x4 slice. The times are simulated.
128 devices in a mesh: sx: 8 (over y, core), sy: 16 (over x, z).
Axes of the slice: x: 4, y: 4, z: 4, core: 2. Of those that a mesh axis runs over, the one named last changes fastest.
Arguments:
- loads: float32 [8, 16, 1536, 256], P('sx', 'sy')
- schur_flex: float32 [8, 16, 1536, 1536], P('sx', 'sy'), as said below
- dirichlet: float32 [8, 16, 1536, 1536], P('sx', 'sy'), as said below
- coupling: float32 [8, 16, 16, 1536], P('sx', 'sy'), may hold values from -0.3125 to 0.3125
- corner_index: int32 [8, 16, 16], P('sx', 'sy'), may hold values from 0 to 512, as said below
- face_lists: int32 [8, 16, 4, 384], P('sx', 'sy'), may hold values from 0 to 383, as said below
- coarse_inverse: float32 [512, 512], P(('sx', 'sy')), as said below
Outputs:
- multipliers: float32 [8, 16, 1536, 256], P('sx', 'sy')
- residual: float32 [8, 16, 1536, 256], P('sx', 'sy')
Inputs may be any that keep to these rules, and one draw needn't show every extreme that they name: `corner_index`: each subdomain lists 4 coarse dofs for each of its four corners; 512 marks a corner on the clamped edges of the panel, which has no coarse dof; every coarse dof below 512 is named by some subdomain. `face_lists`: each face's list is a permutation of the 384 dofs of the facing face; the facing lists of two neighbouring subdomains are inverse permutations. `schur_flex`: symmetric positive definite for every subdomain. `dirichlet`: symmetric positive definite for every subdomain. `coarse_inverse`: symmetric positive definite.
All inputs are finite; a program needn't handle non-finite values.
Results may differ from a plain program's by a relative error of at most 0.00017.
Values sent between devices are 32-bit elements; how exact they have to be, the bound alone decides.
A program may use at most 128 MiB of HBM per device.

v0:
```python
import jax
import jax.numpy as jnp
from jax import lax
from jax.sharding import PartitionSpec as P

ITERS = 2


def shifted(block, axis, distance):
    devices = range(lax.axis_size(axis))
    route = [(i - distance, i) for i in devices if i - distance in devices]
    return lax.ppermute(block, axis, route)


def jump(field, face_index):
    size = field.shape[0] // 4
    width = field.shape[1]
    face_rows = field.reshape(4, size, width)
    from_low_x = shifted(face_rows[1], "sx", 1)
    from_high_x = shifted(face_rows[0], "sx", -1)
    from_low_y = shifted(face_rows[3], "sy", 1)
    from_high_y = shifted(face_rows[2], "sy", -1)
    received = jnp.stack([from_low_x, from_high_x, from_low_y, from_high_y], axis=0)
    matched = received[jnp.arange(4, dtype=jnp.int32)[:, None], face_index]
    return (face_rows - matched).reshape(4 * size, width)


def coarse_solve(coarse_rhs, stiffness_inverse_lines):
    highest = lax.Precision.HIGHEST
    total = lax.psum(coarse_rhs, ("sx", "sy"))
    mine = jnp.dot(stiffness_inverse_lines, total, precision=highest)
    return lax.all_gather(mine, ("sx", "sy"), axis=0, tiled=True)


def inner(first, second):
    return jnp.sum(first * second, axis=0)


def shards(loads, schur_flex, dirichlet, coupling, corner_index, face_lists, coarse_inverse):
    high = lax.Precision.HIGH
    highest = lax.Precision.HIGHEST
    flex_mat = schur_flex[0, 0]
    prec_mat = dirichlet[0, 0]
    coupling_mat = coupling[0, 0]
    corners = corner_index[0, 0]
    face_index = face_lists[0, 0]
    ncoarse = coarse_inverse.shape[1]
    onehot = (corners[None, :] == jnp.arange(ncoarse, dtype=jnp.int32)[:, None]).astype(jnp.float32)
    size = face_index.shape[1]
    sx = lax.axis_index("sx")
    sy = lax.axis_index("sy")
    inside = jnp.stack([sx > 0, sx < lax.axis_size("sx") - 1, sy > 0, sy < lax.axis_size("sy") - 1])
    scale = jnp.repeat(1.0 + inside.astype(jnp.float32), size)[:, None]

    def total(values):
        return lax.psum(values, ("sx", "sy"))

    residual = jump(loads[0, 0], face_index)
    multipliers = jnp.zeros_like(residual)
    direction = None
    residual_inner = None
    for iteration in range(ITERS):
        spread = scale * residual
        operator_applied = jnp.dot(prec_mat, spread, precision=high)
        new_dot = total(0.5 * inner(spread, operator_applied))
        precond = 0.5 * jump(operator_applied, face_index)
        direction = precond if iteration == 0 else precond + new_dot / residual_inner * direction
        residual_inner = new_dot
        apply_spread = scale * direction
        fine_part = jnp.dot(flex_mat, apply_spread, precision=high)
        local_load = jnp.dot(coupling_mat, apply_spread, precision=high)
        coarse_rhs = jnp.dot(onehot, local_load, precision=highest)
        coarse_sol = coarse_solve(coarse_rhs, coarse_inverse)
        filled_out = jnp.concatenate(
            [coarse_sol, jnp.zeros((1, direction.shape[1]), jnp.float32)], axis=0
        )
        picked = filled_out[corners]
        correction = lax.dot_general(coupling_mat, picked, (((0,), (0,)), ((), ())), precision=high)
        applied = fine_part + correction
        step_size = residual_inner / total(inner(apply_spread, applied))
        image_dir = jump(applied, face_index)
        multipliers = multipliers + step_size * direction
        residual = residual - step_size * image_dir
    return (multipliers[None, None], residual[None, None])


def solution(mesh):
    return jax.shard_map(
        shards,
        mesh=mesh,
        in_specs=(
            P("sx", "sy", None, None),
            P("sx", "sy", None, None),
            P("sx", "sy", None, None),
            P("sx", "sy", None, None),
            P("sx", "sy", None),
            P("sx", "sy", None, None),
            P(("sx", "sy"), None),
        ),
        out_specs=(P("sx", "sy", None, None), P("sx", "sy", None, None)),
        check_vma=False,
    )
```

profile of v0, /device:TPU:1, one launch (start us, length us, event | category | flops | bytes accessed | tf_op | source)
XLA Modules:
  0.0 859.2 jit_solution(2950131900494569318)
XLA Ops:
  10.0 5.0 collective-permute-start.2
  27.9 10.7 %gather_fusion = f32[1536,256]{1,0:T(8,128)S(1)} fusion(f32[4,384,256]{2,1,0:T(8,128)S(1)} %pad_maximum_fusion, s32[1536]{0:T(1024)S(1)} %reshape.131), kind=kCustom, calls=%fused_computation | custom fusion | bytes 3158016 | tf_op jit(solution)/shard_map/gather | solution.py:24
  38.6 11.8 %fusion.10 = f32[1536,256]{0,1:T(8,128)S(1)} fusion(f32[1,1,1536,1536]{3,2,1,0:T(8,128)} %param.9, f32[1,1,1536,256]{3,2,1,0:T(8,128)} %param.7, f32[1536,256]{1,0:T(8,128)S(1)} %gather_fusion, f32[1536]{0:T(1024)S(1)} %mul.105), kind=kOutput, calls=%fused_computation.19 | convolution fusion | flops 3624665088 | bytes 14161920 | tf_op jit(solution)/shard_map/dot_general | solution.py:64
  53.4 4.9 collective-permute-start.6
  60.2 4.8 collective-permute-start.4
  74.5 17.9 %gather_fusion.1 = f32[1536,256]{1,0:T(8,128)} fusion(f32[4,384,256]{2,1,0:T(8,128)S(1)} %copy.21, s32[1536]{0:T(1024)S(1)} %reshape.131), kind=kCustom, calls=%fused_computation.1 | custom fusion | bytes 3158016 | tf_op jit(solution)/shard_map/gather | solution.py:24
  100.6 6.7 fusion.2
  107.4 144.9 %all-reduce.6.cloned.1.call-done = f32[512,256]{1,0:T(8,128)} async-done(((f32[512,256]{1,0:T(8,128)}), f32[512,256]{1,0:T(8,128)}) %all-reduce.6.cloned.1.call-update) | async-done | bytes 524304 | tf_op jit(solution)/shard_map/psum | solution.py:30
  253.7 54.1 %all-gather = f32[128,4,256]{2,1,0:T(4,128)} all-gather(f32[1,4,256]{2,1,0:T(4,128)S(1)} %convolution_bitcast_fusion.1), channel_id=1, replica_groups=mesh['sx'=8,'sy'=16] {'sx','sy'}, dimensions={0}, use_global_device_ids=true | all-gather | bytes 528384 | tf_op jit(solution)/shard_map/all_gather | solution.py:32
  317.2 4.0 collective-permute-start.10
  326.8 64.9 %all-reduce.2 = (f32[256]{0:T(256)S(1)}, f32[256]{0:T(256)S(1)}) all-reduce(f32[256]{0:T(256)S(1)} %broadcast_multiply_fusion.3, f32[256]{0:T(256)S(1)} %get-tuple-element.34), channel_id=1, replica_groups=mesh['sx'=8,'sy'=16] {'sx','sy'}, use_global_device_ids=true, to_apply=%region_1.0 | all-reduce | flops 512 | bytes 4096 | tf_op jit(solution)/shard_map/psum | solution.py:56
  396.0 17.9 %gather_fusion.3 = f32[1536,256]{1,0:T(8,128)} fusion(f32[4,384,256]{2,1,0:T(8,128)S(1)} %copy.25, s32[1536]{0:T(1024)S(1)} %reshape.131), kind=kCustom, calls=%fused_computation.3 | custom fusion | bytes 3158016 | tf_op jit(solution)/shard_map/gather | solution.py:24
  419.9 7.5 multiply_reduce_fusion.1
  430.2 4.0 collective-permute-start.14
  434.2 3.4 collective-permute-start.13
  439.8 65.1 %psum.45 = f32[256]{0:T(256)S(1)} all-reduce(f32[256]{0:T(256)S(1)} %broadcast_multiply_fusion.1), channel_id=1, replica_groups=mesh['sx'=8,'sy'=16] {'sx','sy'}, use_global_device_ids=true, to_apply=%region_6.0 | all-reduce | flops 256 | bytes 2048 | tf_op jit(solution)/shard_map/psum | solution.py:56
  509.3 17.9 %gather_fusion.4 = f32[1536,256]{1,0:T(8,128)} fusion(f32[4,384,256]{2,1,0:T(8,128)S(1)} %copy.27, s32[1536]{0:T(1024)S(1)} %reshape.131), kind=kCustom, calls=%fused_computation.4 | custom fusion | bytes 3158016 | tf_op jit(solution)/shard_map/gather | solution.py:24
  534.4 7.7 fusion
  542.2 134.3 %all-reduce.8.cloned.1.call-done = f32[512,256]{1,0:T(8,128)} async-done(((f32[512,256]{1,0:T(8,128)}), f32[512,256]{1,0:T(8,128)}) %all-reduce.8.cloned.1.call-update) | async-done | bytes 524304 | tf_op jit(solution)/shard_map/psum | solution.py:30
  677.9 54.1 %all-gather.1 = f32[128,4,256]{2,1,0:T(4,128)} all-gather(f32[1,4,256]{2,1,0:T(4,128)S(1)} %convolution_bitcast_fusion), channel_id=1, replica_groups=mesh['sx'=8,'sy'=16] {'sx','sy'}, dimensions={0}, use_global_device_ids=true | all-gather | bytes 528384 | tf_op jit(solution)/shard_map/all_gather | solution.py:32
  742.7 4.0 collective-permute-start.18
  752.3 65.2 %psum.47 = f32[256]{0:T(256)S(1)} all-reduce(f32[256]{0:T(256)S(1)} %get-tuple-element.38), channel_id=1, replica_groups=mesh['sx'=8,'sy'=16] {'sx','sy'}, use_global_device_ids=true, to_apply=%region_9.0 | all-reduce | flops 256 | bytes 2048 | tf_op jit(solution)/shard_map/psum | solution.py:56
  821.8 17.9 %gather_fusion.6 = f32[1536,256]{1,0:T(8,128)} fusion(f32[4,384,256]{2,1,0:T(8,128)S(1)} %copy.29, s32[1536]{0:T(1024)S(1)} %reshape.131), kind=kCustom, calls=%fused_computation.6 | custom fusion | bytes 3158016 | tf_op jit(solution)/shard_map/gather | solution.py:24
  842.9 4.8 subtract_bitcast_fusion
  (125 shorter events, 110.8 us)
Async XLA Ops:
  7.2 245.1 %all-reduce.6.cloned.1.call-start = ((), (), s32[]{:S(2)}) async-start(), calls=%async_computation | async-start | bytes 1048576 | tf_op jit(solution)/shard_map/psum | solution.py:30
  8.7 13.2 %collective-permute-start.3 = (f32[384,256]{1,0:T(8,128)S(1)}, f32[384,256]{1,0:T(8,128)S(1)}, u32[]{:S(2)}, u32[]{:S(2)}) collective-permute-start(f32[384,256]{1,0:T(8,128)S(1)} %get-tuple-element.29), channel_id=1, source_target_pairs={{1,0},{2,1},{3,2},{4,3},{5,4},{6,5},{7,6},{8,7},{9,8},{10,9},{11,1... | collective-permute-start | bytes 1179656 | tf_op jit(solution)/shard_map/ppermute | solution.py:12
  10.0 12.8 %collective-permute-start.2 = (f32[384,256]{1,0:T(8,128)S(1)}, f32[384,256]{1,0:T(8,128)S(1)}, u32[]{:S(2)}, u32[]{:S(2)}) collective-permute-start(f32[384,256]{1,0:T(8,128)S(1)} %get-tuple-element.30), channel_id=1, source_target_pairs={{0,1},{1,2},{2,3},{3,4},{4,5},{5,6},{6,7},{7,8},{8,9},{9,10},{10,1... | collective-permute-start | bytes 1179656 | tf_op jit(solution)/shard_map/ppermute | solution.py:12
  15.0 9.6 %collective-permute-start.1 = (f32[384,256]{1,0:T(8,128)S(1)}, f32[384,256]{1,0:T(8,128)S(1)}, u32[]{:S(2)}, u32[]{:S(2)}) collective-permute-start(f32[384,256]{1,0:T(8,128)S(1)} %get-tuple-element.31), channel_id=1, source_target_pairs={{16,0},{32,16},{48,32},{64,48},{80,64},{96,80},{112,96},{17,1},{33... | collective-permute-start | bytes 1179656 | tf_op jit(solution)/shard_map/ppermute | solution.py:12
  17.9 7.9 collective-permute-start
  52.1 16.6 %collective-permute-start.7 = (f32[384,256]{0,1:T(8,128)}, f32[384,256]{0,1:T(8,128)}, u32[]{:S(2)}, u32[]{:S(2)}) collective-permute-start(f32[384,256]{0,1:T(8,128)} %get-tuple-element.25), channel_id=1, source_target_pairs={{1,0},{2,1},{3,2},{4,3},{5,4},{6,5},{7,6},{8,7},{9,8},{10,9},{11,1... | collective-permute-start | bytes 1179656 | tf_op jit(solution)/shard_map/ppermute | solution.py:12
  53.4 15.3 %collective-permute-start.6 = (f32[384,256]{0,1:T(8,128)}, f32[384,256]{0,1:T(8,128)}, u32[]{:S(2)}, u32[]{:S(2)}) collective-permute-start(f32[384,256]{0,1:T(8,128)} %get-tuple-element.26), channel_id=1, source_target_pairs={{0,1},{1,2},{2,3},{3,4},{4,5},{5,6},{6,7},{7,8},{8,9},{9,10},{10,1... | collective-permute-start | bytes 1179656 | tf_op jit(solution)/shard_map/ppermute | solution.py:12
  58.3 10.5 %collective-permute-start.5 = (f32[384,256]{0,1:T(8,128)}, f32[384,256]{0,1:T(8,128)}, u32[]{:S(2)}, u32[]{:S(2)}) collective-permute-start(f32[384,256]{0,1:T(8,128)} %get-tuple-element.27), channel_id=1, source_target_pairs={{16,0},{32,16},{48,32},{64,48},{80,64},{96,80},{112,96},{17,1},{33... | collective-permute-start | bytes 1179656 | tf_op jit(solution)/shard_map/ppermute | solution.py:12
  60.2 9.8 %collective-permute-start.4 = (f32[384,256]{0,1:T(8,128)}, f32[384,256]{0,1:T(8,128)}, u32[]{:S(2)}, u32[]{:S(2)}) collective-permute-start(f32[384,256]{0,1:T(8,128)} %get-tuple-element.24), channel_id=1, source_target_pairs={{0,16},{16,32},{32,48},{48,64},{64,80},{80,96},{96,112},{1,17},{17... | collective-permute-start | bytes 1179656 | tf_op jit(solution)/shard_map/ppermute | solution.py:12
  100.4 151.9 %copy-start.15 = (f32[4,512]{1,0:T(4,128)S(1)}, f32[4,512]{1,0:T(4,128)}, u32[]{:S(2)}) copy-start(f32[4,512]{1,0:T(4,128)} %param.13) | copy-start | bytes 24580
  100.4 576.1 %all-reduce.8.cloned.1.call-start = ((), (), s32[]{:S(2)}) async-start(), calls=%async_computation.1 | async-start | bytes 1048576 | tf_op jit(solution)/shard_map/psum | solution.py:30
  315.9 75.8 %collective-permute-start.11 = (f32[384,256]{0,1:T(8,128)}, f32[384,256]{0,1:T(8,128)S(1)}, u32[]{:S(2)}, u32[]{:S(2)}) collective-permute-start(f32[384,256]{0,1:T(8,128)} %get-tuple-element.21), channel_id=1, source_target_pairs={{1,0},{2,1},{3,2},{4,3},{5,4},{6,5},{7,6},{8,7},{9,8},{10,9},{11,1... | collective-permute-start | bytes 1179656 | tf_op jit(solution)/shard_map/ppermute | solution.py:12
  317.2 74.5 %collective-permute-start.10 = (f32[384,256]{0,1:T(8,128)}, f32[384,256]{0,1:T(8,128)S(1)}, u32[]{:S(2)}, u32[]{:S(2)}) collective-permute-start(f32[384,256]{0,1:T(8,128)} %get-tuple-element.22), channel_id=1, source_target_pairs={{0,1},{1,2},{2,3},{3,4},{4,5},{5,6},{6,7},{7,8},{8,9},{9,10},{10,1... | collective-permute-start | bytes 1179656 | tf_op jit(solution)/shard_map/ppermute | solution.py:12
  321.2 70.5 %collective-permute-start.9 = (f32[384,256]{0,1:T(8,128)S(1)}, f32[384,256]{0,1:T(8,128)}, u32[]{:S(2)}, u32[]{:S(2)}) collective-permute-start(f32[384,256]{0,1:T(8,128)S(1)} %get-tuple-element.23), channel_id=1, source_target_pairs={{16,0},{32,16},{48,32},{64,48},{80,64},{96,80},{112,96},{17,1},{33... | collective-permute-start | bytes 1179656 | tf_op jit(solution)/shard_map/ppermute | solution.py:12
  323.7 68.0 %collective-permute-start.8 = (f32[384,256]{0,1:T(8,128)S(1)}, f32[384,256]{0,1:T(8,128)}, u32[]{:S(2)}, u32[]{:S(2)}) collective-permute-start(f32[384,256]{0,1:T(8,128)S(1)} %get-tuple-element.20), channel_id=1, source_target_pairs={{0,16},{16,32},{32,48},{48,64},{64,80},{80,96},{96,112},{1,17},{17... | collective-permute-start | bytes 1179656 | tf_op jit(solution)/shard_map/ppermute | solution.py:12
  428.9 76.0 %collective-permute-start.15 = (f32[384,256]{0,1:T(8,128)}, f32[384,256]{0,1:T(8,128)S(1)}, u32[]{:S(2)}, u32[]{:S(2)}) collective-permute-start(f32[384,256]{0,1:T(8,128)} %get-tuple-element.15), channel_id=1, source_target_pairs={{1,0},{2,1},{3,2},{4,3},{5,4},{6,5},{7,6},{8,7},{9,8},{10,9},{11,1... | collective-permute-start | bytes 1179656 | tf_op jit(solution)/shard_map/ppermute | solution.py:12
  430.2 74.7 %collective-permute-start.14 = (f32[384,256]{0,1:T(8,128)}, f32[384,256]{0,1:T(8,128)S(1)}, u32[]{:S(2)}, u32[]{:S(2)}) collective-permute-start(f32[384,256]{0,1:T(8,128)} %get-tuple-element.16), channel_id=1, source_target_pairs={{0,1},{1,2},{2,3},{3,4},{4,5},{5,6},{6,7},{7,8},{8,9},{9,10},{10,1... | collective-permute-start | bytes 1179656 | tf_op jit(solution)/shard_map/ppermute | solution.py:12
  434.2 70.7 %collective-permute-start.13 = (f32[384,256]{0,1:T(8,128)S(1)}, f32[384,256]{0,1:T(8,128)}, u32[]{:S(2)}, u32[]{:S(2)}) collective-permute-start(f32[384,256]{0,1:T(8,128)S(1)} %get-tuple-element.17), channel_id=1, source_target_pairs={{16,0},{32,16},{48,32},{64,48},{80,64},{96,80},{112,96},{17,1},{33... | collective-permute-start | bytes 1179656 | tf_op jit(solution)/shard_map/ppermute | solution.py:12
  437.6 67.3 %collective-permute-start.12 = (f32[384,256]{0,1:T(8,128)S(1)}, f32[384,256]{0,1:T(8,128)}, u32[]{:S(2)}, u32[]{:S(2)}) collective-permute-start(f32[384,256]{0,1:T(8,128)S(1)} %get-tuple-element.14), channel_id=1, source_target_pairs={{0,16},{16,32},{32,48},{48,64},{64,80},{80,96},{96,112},{1,17},{17... | collective-permute-start | bytes 1179656 | tf_op jit(solution)/shard_map/ppermute | solution.py:12
  532.4 205.1 %copy-start.1 = (f32[1536,256]{0,1:T(8,128)}, f32[1536,256]{0,1:T(8,128)S(1)}, u32[]{:S(2)}) copy-start(f32[1536,256]{0,1:T(8,128)S(1)} %multiply_add_fusion) | copy-start | bytes 4718596
  741.4 76.0 %collective-permute-start.19 = (f32[384,256]{0,1:T(8,128)}, f32[384,256]{0,1:T(8,128)S(1)}, u32[]{:S(2)}, u32[]{:S(2)}) collective-permute-start(f32[384,256]{0,1:T(8,128)} %get-tuple-element.11), channel_id=1, source_target_pairs={{1,0},{2,1},{3,2},{4,3},{5,4},{6,5},{7,6},{8,7},{9,8},{10,9},{11,1... | collective-permute-start | bytes 1179656 | tf_op jit(solution)/shard_map/ppermute | solution.py:12
  742.7 74.8 %collective-permute-start.18 = (f32[384,256]{0,1:T(8,128)}, f32[384,256]{0,1:T(8,128)S(1)}, u32[]{:S(2)}, u32[]{:S(2)}) collective-permute-start(f32[384,256]{0,1:T(8,128)} %get-tuple-element.12), channel_id=1, source_target_pairs={{0,1},{1,2},{2,3},{3,4},{4,5},{5,6},{6,7},{7,8},{8,9},{9,10},{10,1... | collective-permute-start | bytes 1179656 | tf_op jit(solution)/shard_map/ppermute | solution.py:12
  746.7 70.7 %collective-permute-start.17 = (f32[384,256]{0,1:T(8,128)S(1)}, f32[384,256]{0,1:T(8,128)}, u32[]{:S(2)}, u32[]{:S(2)}) collective-permute-start(f32[384,256]{0,1:T(8,128)S(1)} %get-tuple-element.13), channel_id=1, source_target_pairs={{16,0},{32,16},{48,32},{64,48},{80,64},{96,80},{112,96},{17,1},{33... | collective-permute-start | bytes 1179656 | tf_op jit(solution)/shard_map/ppermute | solution.py:12
  749.2 68.3 %collective-permute-start.16 = (f32[384,256]{0,1:T(8,128)S(1)}, f32[384,256]{0,1:T(8,128)}, u32[]{:S(2)}, u32[]{:S(2)}) collective-permute-start(f32[384,256]{0,1:T(8,128)S(1)} %get-tuple-element.10), channel_id=1, source_target_pairs={{0,16},{16,32},{32,48},{48,64},{64,80},{80,96},{96,112},{1,17},{17... | collective-permute-start | bytes 1179656 | tf_op jit(solution)/shard_map/ppermute | solution.py:12
  (16 other events, 186.9 us)
Sparse Core Ops, SparseCore 0:
  100.5 151.7 all-reduce.5
  534.6 141.8 all-reduce.7
where the time goes:
time: 861 us; the launch traced here: 859 us
  blocking collectives  303 us (35%)
  waiting for transfers between devices  285 us (33%)
  local copies, waits for them, and re-layouts  130 us (15%)
  starting transfers between devices  58.1 us (7%)
  matrix products  44.1 us (5%)
  other arithmetic  24 us (3%)
  between operations  14.6 us (2%)
    psum x2, waiting for transfers between devices, coarse_solve(): total = lax.psum(coarse_rhs, ('sx', 'sy'))  279 us
    psum x3, blocking collectives, total(): return lax.psum(values, ('sx', 'sy'))  195 us
    all_gather x2, blocking collectives, coarse_solve(): return lax.all_gather(mine, ('sx', 'sy'), axis=0, tiled=True)  108 us
    gather x10, local copies, waits for them, and re-layouts, jump(): matched = received[jnp.arange(4, dtype=jnp.int32)[:, None], face_index]  96.4 us
    ppermute x20, starting transfers between devices, shifted(): return lax.ppermute(block, axis, route)  57.8 us
    dot_general x2, matrix products, shards(): operator_applied = jnp.dot(prec_mat, spread, precision=high)  19.4 us
  transfers between devices with their start and end apart: 22, of which 8 were waited for; matrix products, arithmetic and copies ran while one was open for 2% of the time, Pallas kernels for 0%

commit v1 on v0

--- a/solution.py
+++ b/solution.py
@@ -4,6 +4,12 @@
 from jax.sharding import PartitionSpec as P
 
 ITERS = 2
+
+
+def move_trees(local_x, link_axis, row_axis):
+    for hop_no in (link_axis, row_axis):
+        local_x = lax.psum(local_x, hop_no)
+    return local_x
 
 
 def shifted(block, axis, distance):
@@ -53,7 +59,7 @@
     scale = jnp.repeat(1.0 + inside.astype(jnp.float32), size)[:, None]
 
     def total(values):
-        return lax.psum(values, ("sx", "sy"))
+        return move_trees(values, "sx", "sy")
 
     residual = jump(loads[0, 0], face_index)
     multipliers = jnp.zeros_like(residual)

time: 861 us -> 808 us (0.938)
  blocking collectives: 303 us -> 232 us
    psum x3 -> x6, blocking collectives: 195 us -> 124 us  [move_trees(): local_x = lax.psum(local_x, hop_no)]
where the time goes in v1:
time: 808 us; the launch traced here: 800 us
  waiting for transfers between devices  289 us (36%)
  blocking collectives  232 us (29%)
  local copies, waits for them, and re-layouts  130 us (16%)
  starting transfers between devices  65.8 us (8%)
  matrix products  44.1 us (5%)
  other arithmetic  24 us (3%)
  between operations  14.6 us (2%)
    psum x2, waiting for transfers between devices, coarse_solve(): total = lax.psum(coarse_rhs, ('sx', 'sy'))  283 us
    psum x6, blocking collectives, move_trees(): local_x = lax.psum(local_x, hop_no)  124 us
    all_gather x2, blocking collectives, coarse_solve(): return lax.all_gather(mine, ('sx', 'sy'), axis=0, tiled=True)  108 us
    gather x10, local copies, waits for them, and re-layouts, jump(): matched = received[jnp.arange(4, dtype=jnp.int32)[:, None], face_index]  96.3 us
    ppermute x20, starting transfers between devices, shifted(): return lax.ppermute(block, axis, route)  65.5 us
    dot_general x2, matrix products, shards(): operator_applied = jnp.dot(prec_mat, spread, precision=high)  19.4 us
  transfers between devices with their start and end apart: 22, of which 8 were waited for; matrix products, arithmetic and copies ran while one was open for 2% of the time, Pallas kernels for 0%

profile of v1, /device:TPU:1, one launch (start us, length us, event | category | flops | bytes accessed | tf_op | source)
XLA Modules:
  0.0 799.6 jit_solution(2014983860255474838)
XLA Ops:
  10.0 5.0 collective-permute-start.2
  27.9 10.7 %gather_fusion = f32[1536,256]{1,0:T(8,128)S(1)} fusion(f32[4,384,256]{2,1,0:T(8,128)S(1)} %pad_maximum_fusion, s32[1536]{0:T(1024)S(1)} %reshape.131), kind=kCustom, calls=%fused_computation | custom fusion | bytes 3158016 | tf_op jit(solution)/shard_map/gather | solution.py:30
  38.6 11.8 %fusion.10 = f32[1536,256]{0,1:T(8,128)S(1)} fusion(f32[1,1,1536,1536]{3,2,1,0:T(8,128)} %param.9, f32[1,1,1536,256]{3,2,1,0:T(8,128)} %param.7, f32[1536,256]{1,0:T(8,128)S(1)} %gather_fusion, f32[1536]{0:T(1024)S(1)} %mul.105), kind=kOutput, calls=%fused_computation.19 | convolution fusion | flops 3624665088 | bytes 14161920 | tf_op jit(solution)/shard_map/dot_general | solution.py:70
  53.4 4.9 collective-permute-start.6
  60.2 4.8 collective-permute-start.4
  74.5 17.9 %gather_fusion.1 = f32[1536,256]{1,0:T(8,128)} fusion(f32[4,384,256]{2,1,0:T(8,128)S(1)} %copy.21, s32[1536]{0:T(1024)S(1)} %reshape.131), kind=kCustom, calls=%fused_computation.1 | custom fusion | bytes 3158016 | tf_op jit(solution)/shard_map/gather | solution.py:30
  100.6 6.7 fusion.2
  107.4 144.9 %all-reduce.7.cloned.1.call-done = f32[512,256]{1,0:T(8,128)} async-done(((f32[512,256]{1,0:T(8,128)}), f32[512,256]{1,0:T(8,128)}) %all-reduce.7.cloned.1.call-update) | async-done | bytes 524304 | tf_op jit(solution)/shard_map/psum | solution.py:36
  253.6 54.1 %all-gather = f32[128,4,256]{2,1,0:T(4,128)} all-gather(f32[1,4,256]{2,1,0:T(4,128)S(1)} %convolution_bitcast_fusion.1), channel_id=1, replica_groups=mesh['sx'=8,'sy'=16] {'sx','sy'}, dimensions={0}, use_global_device_ids=true | all-gather | bytes 528384 | tf_op jit(solution)/shard_map/all_gather | solution.py:38
  326.7 11.8 %all-reduce.3 = (f32[256]{0:T(256)S(1)}, f32[256]{0:T(256)S(1)}) all-reduce(f32[256]{0:T(256)S(1)} %broadcast_multiply_fusion.3, f32[256]{0:T(256)S(1)} %get-tuple-element.36), channel_id=1, replica_groups=mesh['sx'=8,'sy'=16] {'sx'}, use_global_device_ids=true, to_apply=%region_1.0 | all-reduce | flops 512 | bytes 4096 | tf_op jit(solution)/shard_map/psum | solution.py:11
  338.5 28.6 %all-reduce.2 = (f32[256]{0:T(256)S(1)}, f32[256]{0:T(256)S(1)}) all-reduce(f32[256]{0:T(256)S(1)} %get-tuple-element.8, f32[256]{0:T(256)S(1)} %get-tuple-element.9), channel_id=1, replica_groups=mesh['sx'=8,'sy'=16] {'sy'}, use_global_device_ids=true, to_apply=%region_2.0 | all-reduce | flops 512 | bytes 4096 | tf_op jit(solution)/shard_map/psum | solution.py:11
  371.4 17.9 %gather_fusion.3 = f32[1536,256]{1,0:T(8,128)} fusion(f32[4,384,256]{2,1,0:T(8,128)S(1)} %copy.25, s32[1536]{0:T(1024)S(1)} %reshape.131), kind=kCustom, calls=%fused_computation.3 | custom fusion | bytes 3158016 | tf_op jit(solution)/shard_map/gather | solution.py:30
  395.3 7.5 multiply_reduce_fusion.1
  409.7 11.2 %collective-permute-start.13 = (f32[384,256]{0,1:T(8,128)S(1)}, f32[384,256]{0,1:T(8,128)}, u32[]{:S(2)}, u32[]{:S(2)}) collective-permute-start(f32[384,256]{0,1:T(8,128)S(1)} %get-tuple-element.19), channel_id=1, source_target_pairs={{16,0},{32,16},{48,32},{64,48},{80,64},{96,80},{112,96},{17,1},{33... | collective-permute-start | bytes 1179656 | tf_op jit(solution)/shard_map/ppermute | solution.py:18
  422.9 13.0 %psum.75 = f32[256]{0:T(256)S(1)} all-reduce(f32[256]{0:T(256)S(1)} %broadcast_multiply_fusion.1), channel_id=1, replica_groups=mesh['sx'=8,'sy'=16] {'sx'}, use_global_device_ids=true, to_apply=%region_8.0 | all-reduce | flops 256 | bytes 2048 | tf_op jit(solution)/shard_map/psum | solution.py:11
  435.9 30.0 %psum.76 = f32[256]{0:T(256)S(1)} all-reduce(f32[256]{0:T(256)S(1)} %psum.75), channel_id=1, replica_groups=mesh['sx'=8,'sy'=16] {'sy'}, use_global_device_ids=true, to_apply=%region_9.0 | all-reduce | flops 256 | bytes 2048 | tf_op jit(solution)/shard_map/psum | solution.py:11
  470.2 17.9 %gather_fusion.4 = f32[1536,256]{1,0:T(8,128)} fusion(f32[4,384,256]{2,1,0:T(8,128)S(1)} %copy.27, s32[1536]{0:T(1024)S(1)} %reshape.131), kind=kCustom, calls=%fused_computation.4 | custom fusion | bytes 3158016 | tf_op jit(solution)/shard_map/gather | solution.py:30
  495.3 7.7 fusion
  503.0 138.6 %all-reduce.9.cloned.1.call-done = f32[512,256]{1,0:T(8,128)} async-done(((f32[512,256]{1,0:T(8,128)}), f32[512,256]{1,0:T(8,128)}) %all-reduce.9.cloned.1.call-update) | async-done | bytes 524304 | tf_op jit(solution)/shard_map/psum | solution.py:36
  643.0 54.1 %all-gather.1 = f32[128,4,256]{2,1,0:T(4,128)} all-gather(f32[1,4,256]{2,1,0:T(4,128)S(1)} %convolution_bitcast_fusion), channel_id=1, replica_groups=mesh['sx'=8,'sy'=16] {'sx','sy'}, dimensions={0}, use_global_device_ids=true | all-gather | bytes 528384 | tf_op jit(solution)/shard_map/all_gather | solution.py:38
  717.5 11.8 %psum.78 = f32[256]{0:T(256)S(1)} all-reduce(f32[256]{0:T(256)S(1)} %get-tuple-element.40), channel_id=1, replica_groups=mesh['sx'=8,'sy'=16] {'sx'}, use_global_device_ids=true, to_apply=%region_12.0 | all-reduce | flops 256 | bytes 2048 | tf_op jit(solution)/shard_map/psum | solution.py:11
  729.3 28.6 %psum.79 = f32[256]{0:T(256)S(1)} all-reduce(f32[256]{0:T(256)S(1)} %psum.78), channel_id=1, replica_groups=mesh['sx'=8,'sy'=16] {'sy'}, use_global_device_ids=true, to_apply=%region_13.0 | all-reduce | flops 256 | bytes 2048 | tf_op jit(solution)/shard_map/psum | solution.py:11
  762.2 17.9 %gather_fusion.6 = f32[1536,256]{1,0:T(8,128)} fusion(f32[4,384,256]{2,1,0:T(8,128)S(1)} %copy.29, s32[1536]{0:T(1024)S(1)} %reshape.131), kind=kCustom, calls=%fused_computation.6 | custom fusion | bytes 3158016 | tf_op jit(solution)/shard_map/gather | solution.py:30
  783.2 4.7 subtract_bitcast_fusion
  (128 shorter events, 122.5 us)
Async XLA Ops:
  7.2 245.1 %all-reduce.7.cloned.1.call-start = ((), (), s32[]{:S(2)}) async-start(), calls=%async_computation | async-start | bytes 1048576 | tf_op jit(solution)/shard_map/psum | solution.py:36
  8.7 13.2 %collective-permute-start.3 = (f32[384,256]{1,0:T(8,128)S(1)}, f32[384,256]{1,0:T(8,128)S(1)}, u32[]{:S(2)}, u32[]{:S(2)}) collective-permute-start(f32[384,256]{1,0:T(8,128)S(1)} %get-tuple-element.31), channel_id=1, source_target_pairs={{1,0},{2,1},{3,2},{4,3},{5,4},{6,5},{7,6},{8,7},{9,8},{10,9},{11,1... | collective-permute-start | bytes 1179656 | tf_op jit(solution)/shard_map/ppermute | solution.py:18
  10.0 12.8 %collective-permute-start.2 = (f32[384,256]{1,0:T(8,128)S(1)}, f32[384,256]{1,0:T(8,128)S(1)}, u32[]{:S(2)}, u32[]{:S(2)}) collective-permute-start(f32[384,256]{1,0:T(8,128)S(1)} %get-tuple-element.32), channel_id=1, source_target_pairs={{0,1},{1,2},{2,3},{3,4},{4,5},{5,6},{6,7},{7,8},{8,9},{9,10},{10,1... | collective-permute-start | bytes 1179656 | tf_op jit(solution)/shard_map/ppermute | solution.py:18
  15.0 9.6 %collective-permute-start.1 = (f32[384,256]{1,0:T(8,128)S(1)}, f32[384,256]{1,0:T(8,128)S(1)}, u32[]{:S(2)}, u32[]{:S(2)}) collective-permute-start(f32[384,256]{1,0:T(8,128)S(1)} %get-tuple-element.33), channel_id=1, source_target_pairs={{16,0},{32,16},{48,32},{64,48},{80,64},{96,80},{112,96},{17,1},{33... | collective-permute-start | bytes 1179656 | tf_op jit(solution)/shard_map/ppermute | solution.py:18
  17.9 7.9 collective-permute-start
  52.1 16.6 %collective-permute-start.7 = (f32[384,256]{0,1:T(8,128)}, f32[384,256]{0,1:T(8,128)}, u32[]{:S(2)}, u32[]{:S(2)}) collective-permute-start(f32[384,256]{0,1:T(8,128)} %get-tuple-element.27), channel_id=1, source_target_pairs={{1,0},{2,1},{3,2},{4,3},{5,4},{6,5},{7,6},{8,7},{9,8},{10,9},{11,1... | collective-permute-start | bytes 1179656 | tf_op jit(solution)/shard_map/ppermute | solution.py:18
  53.4 15.3 %collective-permute-start.6 = (f32[384,256]{0,1:T(8,128)}, f32[384,256]{0,1:T(8,128)}, u32[]{:S(2)}, u32[]{:S(2)}) collective-permute-start(f32[384,256]{0,1:T(8,128)} %get-tuple-element.28), channel_id=1, source_target_pairs={{0,1},{1,2},{2,3},{3,4},{4,5},{5,6},{6,7},{7,8},{8,9},{9,10},{10,1... | collective-permute-start | bytes 1179656 | tf_op jit(solution)/shard_map/ppermute | solution.py:18
  58.3 10.5 %collective-permute-start.5 = (f32[384,256]{0,1:T(8,128)}, f32[384,256]{0,1:T(8,128)}, u32[]{:S(2)}, u32[]{:S(2)}) collective-permute-start(f32[384,256]{0,1:T(8,128)} %get-tuple-element.29), channel_id=1, source_target_pairs={{16,0},{32,16},{48,32},{64,48},{80,64},{96,80},{112,96},{17,1},{33... | collective-permute-start | bytes 1179656 | tf_op jit(solution)/shard_map/ppermute | solution.py:18
  60.2 9.8 %collective-permute-start.4 = (f32[384,256]{0,1:T(8,128)}, f32[384,256]{0,1:T(8,128)}, u32[]{:S(2)}, u32[]{:S(2)}) collective-permute-start(f32[384,256]{0,1:T(8,128)} %get-tuple-element.26), channel_id=1, source_target_pairs={{0,16},{16,32},{32,48},{48,64},{64,80},{80,96},{96,112},{1,17},{17... | collective-permute-start | bytes 1179656 | tf_op jit(solution)/shard_map/ppermute | solution.py:18
  100.4 151.9 %copy-start.15 = (f32[4,512]{1,0:T(4,128)S(1)}, f32[4,512]{1,0:T(4,128)}, u32[]{:S(2)}) copy-start(f32[4,512]{1,0:T(4,128)} %param.13) | copy-start | bytes 24580
  100.4 541.2 %all-reduce.9.cloned.1.call-start = ((), (), s32[]{:S(2)}) async-start(), calls=%async_computation.1 | async-start | bytes 1048576 | tf_op jit(solution)/shard_map/psum | solution.py:36
  315.8 51.3 %collective-permute-start.11 = (f32[384,256]{0,1:T(8,128)}, f32[384,256]{0,1:T(8,128)S(1)}, u32[]{:S(2)}, u32[]{:S(2)}) collective-permute-start(f32[384,256]{0,1:T(8,128)} %get-tuple-element.23), channel_id=1, source_target_pairs={{1,0},{2,1},{3,2},{4,3},{5,4},{6,5},{7,6},{8,7},{9,8},{10,9},{11,1... | collective-permute-start | bytes 1179656 | tf_op jit(solution)/shard_map/ppermute | solution.py:18
  317.1 50.0 %collective-permute-start.10 = (f32[384,256]{0,1:T(8,128)}, f32[384,256]{0,1:T(8,128)S(1)}, u32[]{:S(2)}, u32[]{:S(2)}) collective-permute-start(f32[384,256]{0,1:T(8,128)} %get-tuple-element.24), channel_id=1, source_target_pairs={{0,1},{1,2},{2,3},{3,4},{4,5},{5,6},{6,7},{7,8},{8,9},{9,10},{10,1... | collective-permute-start | bytes 1179656 | tf_op jit(solution)/shard_map/ppermute | solution.py:18
  321.1 46.0 %collective-permute-start.9 = (f32[384,256]{0,1:T(8,128)S(1)}, f32[384,256]{0,1:T(8,128)}, u32[]{:S(2)}, u32[]{:S(2)}) collective-permute-start(f32[384,256]{0,1:T(8,128)S(1)} %get-tuple-element.25), channel_id=1, source_target_pairs={{16,0},{32,16},{48,32},{64,48},{80,64},{96,80},{112,96},{17,1},{33... | collective-permute-start | bytes 1179656 | tf_op jit(solution)/shard_map/ppermute | solution.py:18
  323.6 43.5 %collective-permute-start.8 = (f32[384,256]{0,1:T(8,128)S(1)}, f32[384,256]{0,1:T(8,128)}, u32[]{:S(2)}, u32[]{:S(2)}) collective-permute-start(f32[384,256]{0,1:T(8,128)S(1)} %get-tuple-element.22), channel_id=1, source_target_pairs={{0,16},{16,32},{32,48},{48,64},{64,80},{80,96},{96,112},{1,17},{17... | collective-permute-start | bytes 1179656 | tf_op jit(solution)/shard_map/ppermute | solution.py:18
  404.3 61.5 %collective-permute-start.15 = (f32[384,256]{0,1:T(8,128)}, f32[384,256]{0,1:T(8,128)S(1)}, u32[]{:S(2)}, u32[]{:S(2)}) collective-permute-start(f32[384,256]{0,1:T(8,128)} %get-tuple-element.17), channel_id=1, source_target_pairs={{1,0},{2,1},{3,2},{4,3},{5,4},{6,5},{7,6},{8,7},{9,8},{10,9},{11,1... | collective-permute-start | bytes 1179656 | tf_op jit(solution)/shard_map/ppermute | solution.py:18
  405.6 60.3 %collective-permute-start.14 = (f32[384,256]{0,1:T(8,128)}, f32[384,256]{0,1:T(8,128)S(1)}, u32[]{:S(2)}, u32[]{:S(2)}) collective-permute-start(f32[384,256]{0,1:T(8,128)} %get-tuple-element.18), channel_id=1, source_target_pairs={{0,1},{1,2},{2,3},{3,4},{4,5},{5,6},{6,7},{7,8},{8,9},{9,10},{10,1... | collective-permute-start | bytes 1179656 | tf_op jit(solution)/shard_map/ppermute | solution.py:18
  409.7 56.2 %collective-permute-start.13 = (f32[384,256]{0,1:T(8,128)S(1)}, f32[384,256]{0,1:T(8,128)}, u32[]{:S(2)}, u32[]{:S(2)}) collective-permute-start(f32[384,256]{0,1:T(8,128)S(1)} %get-tuple-element.19), channel_id=1, source_target_pairs={{16,0},{32,16},{48,32},{64,48},{80,64},{96,80},{112,96},{17,1},{33... | collective-permute-start | bytes 1179656 | tf_op jit(solution)/shard_map/ppermute | solution.py:18
  421.0 44.9 %collective-permute-start.12 = (f32[384,256]{0,1:T(8,128)S(1)}, f32[384,256]{0,1:T(8,128)}, u32[]{:S(2)}, u32[]{:S(2)}) collective-permute-start(f32[384,256]{0,1:T(8,128)S(1)} %get-tuple-element.16), channel_id=1, source_target_pairs={{0,16},{16,32},{32,48},{48,64},{64,80},{80,96},{96,112},{1,17},{17... | collective-permute-start | bytes 1179656 | tf_op jit(solution)/shard_map/ppermute | solution.py:18
  493.3 209.3 %copy-start.1 = (f32[1536,256]{0,1:T(8,128)}, f32[1536,256]{0,1:T(8,128)S(1)}, u32[]{:S(2)}) copy-start(f32[1536,256]{0,1:T(8,128)S(1)} %multiply_add_fusion) | copy-start | bytes 4718596
  706.6 51.3 %collective-permute-start.19 = (f32[384,256]{0,1:T(8,128)}, f32[384,256]{0,1:T(8,128)S(1)}, u32[]{:S(2)}, u32[]{:S(2)}) collective-permute-start(f32[384,256]{0,1:T(8,128)} %get-tuple-element.13), channel_id=1, source_target_pairs={{1,0},{2,1},{3,2},{4,3},{5,4},{6,5},{7,6},{8,7},{9,8},{10,9},{11,1... | collective-permute-start | bytes 1179656 | tf_op jit(solution)/shard_map/ppermute | solution.py:18
  707.9 50.0 %collective-permute-start.18 = (f32[384,256]{0,1:T(8,128)}, f32[384,256]{0,1:T(8,128)S(1)}, u32[]{:S(2)}, u32[]{:S(2)}) collective-permute-start(f32[384,256]{0,1:T(8,128)} %get-tuple-element.14), channel_id=1, source_target_pairs={{0,1},{1,2},{2,3},{3,4},{4,5},{5,6},{6,7},{7,8},{8,9},{9,10},{10,1... | collective-permute-start | bytes 1179656 | tf_op jit(solution)/shard_map/ppermute | solution.py:18
  711.9 46.0 %collective-permute-start.17 = (f32[384,256]{0,1:T(8,128)S(1)}, f32[384,256]{0,1:T(8,128)}, u32[]{:S(2)}, u32[]{:S(2)}) collective-permute-start(f32[384,256]{0,1:T(8,128)S(1)} %get-tuple-element.15), channel_id=1, source_target_pairs={{16,0},{32,16},{48,32},{64,48},{80,64},{96,80},{112,96},{17,1},{33... | collective-permute-start | bytes 1179656 | tf_op jit(solution)/shard_map/ppermute | solution.py:18
  714.3 43.5 %collective-permute-start.16 = (f32[384,256]{0,1:T(8,128)S(1)}, f32[384,256]{0,1:T(8,128)}, u32[]{:S(2)}, u32[]{:S(2)}) collective-permute-start(f32[384,256]{0,1:T(8,128)S(1)} %get-tuple-element.12), channel_id=1, source_target_pairs={{0,16},{16,32},{32,48},{48,64},{64,80},{80,96},{96,112},{1,17},{17... | collective-permute-start | bytes 1179656 | tf_op jit(solution)/shard_map/ppermute | solution.py:18
  (16 other events, 186.9 us)
Sparse Core Ops, SparseCore 0:
  100.5 151.6 all-reduce.6
  495.4 146.1 all-reduce.8
